TPU v7x, 32 devices: a whole 2x2x4 slice. The times are simulated.
32 devices in a mesh: grp: 4 (over y, x), dev: 8 (over z, core).
Axes of the slice: x: 2, y: 2, z: 4, core: 2. Of those that a mesh axis runs over, the one named last changes fastest.
Arguments:
- q_lat: bfloat16 [128, 64, 576], P(('grp', 'dev')), parts along dimension 0, may hold values from -40 to 40
- latent_cache: bfloat16 [128, 256, 576], P(('grp', 'dev')), parts along dimension 0, may hold values from -8 to 8
- lengths: int32 [128], P('grp'), parts along dimension 0, may hold values from 32 to 256, as said below
- moves: int32 [64, 3], P('grp'), parts along dimension 0, may hold values from 0 to 31, as said below
- hidden_in: bfloat16 [128, 3584], P(('grp', 'dev')), parts along dimension 0, may hold values from -6 to 6
- norm_gain: bfloat16 [3584], replicated, may hold values from 0.25 to 1.75
- w_up: bfloat16 [3584, 10240], P(None, 'dev'), may hold values from -0.09375 to 0.09375
- w_down: bfloat16 [10240, 3584], P('dev'), may hold values from -0.0625 to 0.0625
- queue_counts: int32 [32, 8], P(('grp', 'dev')), parts along dimension 0, may hold values from 0 to 63
- deadline: int32 [128], P(('grp', 'dev')), parts along dimension 0, may hold values from 0 to 7
Outputs:
- attn_out: bfloat16 [128, 64, 512], P(('grp', 'dev')), parts along dimension 0
- new_cache: bfloat16 [128, 256, 576], P(('grp', 'dev')), parts along dimension 0
- mixed: bfloat16 [128, 3584], P(('grp', 'dev')), parts along dimension 0
- bucket_load: float32 [32], P('grp'), parts along dimension 0
There are 4 independent parts, one for each index of `grp`. A program takes and returns all parts, laid end to end along the dimension named above; an argument that names none is the same for every part. Nothing has to cross between parts.
Inputs may be any that keep to these rules, and one draw needn't show every extreme that they name: `lengths`: every length is at least 32; some request has exactly 256. `moves`: entry j * 8 + s (j below 2) has source device s and names a request of device s (requests r lie on device r // 4); the requests listed for one device are distinct. In round j every source s sends to (s + k_j) mod 8, with k_j between 1 and 7 the same for all sources of the round and different between rounds; one of the rounds has k_j = 4.
All inputs are finite; a program needn't handle non-finite values.
Results may differ from a plain program's by a relative error of at most 0.002.
The roundings to bfloat16 on the way count: a program that leaves them out, or rounds other values in their place, can miss the bound.
Values may be sent and summed in bfloat16 or wider, within the bound.
A program may use at most 128 MiB of HBM per device.

v0:
```python
from functools import partial
import jax
import jax.numpy as jnp
from jax import lax
from jax.sharding import PartitionSpec as P

VL = 512
MOVE_DEV = 2
BUCKETS = 8
softmax_scale = 192.0 ** (-0.5)


def for_sending(x):

    def short(part):
        return part.astype(jnp.bfloat16) if part.dtype == jnp.float32 else part

    return jax.tree.map(short, x)


def shifted(value, axis, steps):
    count = lax.axis_size(axis)
    pairs = [(source, (source + steps) % count) for source in range(count)]
    return lax.ppermute(value, axis, pairs)


def attend(queries, latent, context_lengths):
    row_count = queries.shape[0]
    head_count = queries.shape[1]
    block_size = min(128, latent.shape[1])
    block_count = (jnp.max(context_lengths) + block_size - 1) // block_size
    initial = (
        jnp.full((row_count, head_count), -1e30, jnp.float32),
        jnp.zeros((row_count, head_count), jnp.float32),
        jnp.zeros((row_count, head_count, VL), jnp.float32),
    )

    def advance(block_index, carried):
        running_max, running_sum, accumulated = carried
        key_block = lax.dynamic_slice_in_dim(latent, block_index * block_size, block_size, 1)
        scores = (
            jnp.einsum("rhc,rkc->rhk", queries, key_block, preferred_element_type=jnp.float32)
            * softmax_scale
        )
        positions = block_index * block_size + jnp.arange(block_size, dtype=jnp.int32)
        included = positions[None, None, :] < context_lengths[:, None, None]
        scores = jnp.where(included, scores, jnp.float32(-1e30))
        new_max = jnp.maximum(running_max, jnp.max(scores, axis=-1))
        factor = jnp.exp(running_max - new_max)
        weights = jnp.where(included, jnp.exp(scores - new_max[:, :, None]), jnp.float32(0.0))
        running_sum = running_sum * factor + jnp.sum(weights, axis=-1)
        product = jnp.einsum(
            "rhk,rkc->rhc",
            weights.astype(jnp.bfloat16),
            key_block[:, :, :VL],
            preferred_element_type=jnp.float32,
        )
        accumulated = accumulated * factor[:, :, None] + product
        return (new_max, running_sum, accumulated)

    final_max, final_sum, accumulated = lax.fori_loop(0, block_count, advance, initial)
    return (accumulated / final_sum[:, :, None]).astype(jnp.bfloat16)


def moved_by(offset, single_row):
    return jax.tree.map(
        lambda part, own: part.astype(own.dtype),
        shifted(for_sending(single_row), "dev", offset),
        single_row,
    )


def send_round(single_row, round_distance, devices):
    branches = [partial(moved_by, offset) for offset in range(1, devices)]
    return lax.switch(round_distance - 1, branches, single_row)


def per_device(
    q_lat, latent_cache, lengths, moves, hidden_in, norm_gain, w_up, w_down, queue_counts, deadline
):
    devices = lax.axis_size("dev")
    my_index = lax.axis_index("dev")
    row_count = latent_cache.shape[0]
    context = latent_cache.shape[1]
    rounds = moves.reshape(MOVE_DEV, devices, 3)
    own_moves = rounds[:, my_index, :]
    leaving = own_moves[:, 0] - my_index * row_count
    distance = (own_moves[:, 2] - my_index) % devices
    own_lengths = lax.dynamic_slice_in_dim(lengths, my_index * row_count, row_count)
    payload = latent_cache[leaving]
    arrivals = []
    for round_index in range(MOVE_DEV):
        arrivals.append(send_round(payload[round_index], distance[round_index], devices))
    travelled = jnp.stack(arrivals, axis=0)
    new_cache = latent_cache.at[leaving].set(travelled[:, :context])
    attn_out = attend(q_lat, latent_cache, own_lengths)
    widened = hidden_in.astype(jnp.float32)
    scaled = lax.rsqrt(jnp.mean(widened * widened, axis=-1, keepdims=True) + 1e-06)
    normed = (widened * scaled * norm_gain.astype(jnp.float32)[None, :]).astype(jnp.bfloat16)
    running = (deadline[:, None] == jnp.arange(BUCKETS, dtype=jnp.int32)[None, :]).astype(
        jnp.float32
    )
    bucket_terms = queue_counts.astype(jnp.float32)[0] + jnp.sum(running, axis=0)
    all_rows = lax.all_gather(normed, "dev", axis=0, tiled=True)
    bucket_load = lax.psum(bucket_terms, "dev")
    hidden_units = jax.nn.silu(jnp.dot(all_rows, w_up, preferred_element_type=jnp.float32)).astype(
        jnp.bfloat16
    )
    partial_sum = lax.psum_scatter(
        jnp.dot(hidden_units, w_down, preferred_element_type=jnp.float32),
        "dev",
        scatter_dimension=0,
        tiled=True,
    )
    mixed = (widened + partial_sum).astype(jnp.bfloat16)
    return (attn_out, new_cache, mixed, bucket_load)


def solution(mesh):
    return jax.shard_map(
        per_device,
        mesh=mesh,
        in_specs=(
            P(("grp", "dev"), None, None),
            P(("grp", "dev"), None, None),
            P("grp"),
            P("grp", None),
            P(("grp", "dev"), None),
            P(),
            P(None, "dev"),
            P("dev", None),
            P(("grp", "dev"), None),
            P(("grp", "dev")),
        ),
        out_specs=(
            P(("grp", "dev"), None, None),
            P(("grp", "dev"), None, None),
            P(("grp", "dev"), None),
            P("grp"),
        ),
        check_vma=False,
    )
```

profile of v0, /device:TPU:0, one launch (start us, length us, event | category | flops | bytes accessed | tf_op | source)
XLA Modules:
  0.0 112.7 jit_solution(7425908061489002161)
XLA Ops:
  7.2 0.0 copy-start.3
  7.2 0.0 copy-start.4
  7.2 0.0 all-reduce.3.cloned.1.call-start
  7.2 0.6 copy-done.4
  7.9 0.0 copy-done.3
  7.9 0.1 fusion.15
  8.1 0.1 fusion.19
  8.2 16.0 %all-gather = bf16[8,4,3584]{2,1,0:T(4,128)(2,1)S(1)} all-gather(bf16[1,4,3584]{2,1,0:T(4,128)(2,1)S(1)} %fusion.19), channel_id=1, replica_groups=mesh['grp'=4,'dev'=8] {'dev'}, dimensions={0}, use_global_device_ids=true | all-gather | bytes 258048 | tf_op jit(solution)/shard_map/all_gather | solution.py:104
  24.1 0.1 reshape.87
  24.2 0.0 copy-start.6
  24.2 0.0 copy-start.1
  24.2 0.0 copy-start.2
  24.2 10.4 %fusion.13 = f32[32,3584]{1,0:T(8,128)} fusion(bf16[1280,3584]{1,0:T(8,128)(2,1)} %param.33, bf16[32,3584]{1,0:T(8,128)(2,1)S(1)} %reshape.87, bf16[3584,1280]{1,0:T(8,128)(2,1)} %param.32), kind=kOutput, calls=%fused_computation.41 | convolution fusion | flops 587407360 | bytes 19038208 | tf_op jit(solution)/shard_map/dot_general | solution.py:110
  34.7 0.0 all-reduce.3.cloned.1.call-update
  34.7 0.0 copy-done.6
  34.7 0.7 fusion.23
  36.1 0.1 broadcast_in_dim.42
  36.2 0.0 copy-start.5
  36.2 1.0 while.14
  36.2 0.1 broadcast_compare_fusion.2
  36.3 0.3 fusion.40
  36.7 0.2 fusion.41
  36.9 0.4 convolution_add_fusion.2
  37.3 0.1 reshape.69
  37.3 0.1 constant_dynamic-slice_fusion
  37.4 0.1 copy.52
  37.5 0.2 subtract_reduce_fusion
  37.7 0.6 fusion.25
  38.3 0.6 gather_fusion
  38.9 0.3 copy.53
  40.5 16.7 %conditional.3 = (bf16[1,256,576]{2,1,0:T(8,128)(2,1)}) conditional(s32[]{:T(128)} %bitcast.31, bf16[2,256,576]{2,1,0:T(8,128)(2,1)S(1)} %copy.53, bf16[2,256,576]{2,1,0:T(8,128)(2,1)S(1)} %copy.53, bf16[2,256,576]{2,1,0:T(8,128)(2,1)S(1)} %copy.53, bf16[2,256,576]{2,1,0:T(8,128)(2,1)S(1)} %copy.53, ...), branch_computations={%region_12.13_spmd, %region_13.14_spmd, %region_14.15_spmd, %regio... | conditional | bytes 1769520 | solution.py:75
  40.6 2.5 %collective-permute-start.9 = (bf16[256,576]{1,0:T(8,128)(2,1)S(1)}, bf16[256,576]{1,0:T(8,128)(2,1)}, u32[]{:S(2)}, u32[]{:S(2)}) collective-permute-start(bf16[256,576]{1,0:T(8,128)(2,1)S(1)} %slice_bitcast_fusion.9), channel_id=1, source_target_pairs={{0,3},{1,4},{2,5},{3,6},{4,7},{5,0},{6,1},{7,2},{8,11},{9,12},{10,... | collective-permute-start | bytes 884744 | tf_op jit(solution)/shard_map/cond/branch_2_fun/ppermute | solution.py:24
  43.1 14.1 %collective-permute-done.9 = bf16[256,576]{1,0:T(8,128)(2,1)} collective-permute-done((bf16[256,576]{1,0:T(8,128)(2,1)S(1)}, bf16[256,576]{1,0:T(8,128)(2,1)}, u32[]{:S(2)}, u32[]{:S(2)}) %collective-permute-start.9) | collective-permute-done | bytes 294944 | tf_op jit(solution)/shard_map/cond/branch_2_fun/ppermute | solution.py:24
  57.2 16.8 %conditional.2 = (bf16[1,256,576]{2,1,0:T(8,128)(2,1)}) conditional(s32[]{:T(128)} %bitcast.30, bf16[2,256,576]{2,1,0:T(8,128)(2,1)S(1)} %copy.53, bf16[2,256,576]{2,1,0:T(8,128)(2,1)S(1)} %copy.53, bf16[2,256,576]{2,1,0:T(8,128)(2,1)S(1)} %copy.53, bf16[2,256,576]{2,1,0:T(8,128)(2,1)S(1)} %copy.53, ...), branch_computations={%region_5.6_spmd, %region_6.7_spmd, %region_7.8_spmd, %region_8.9_... | conditional | bytes 1769520 | solution.py:75
  57.3 0.1 collective-permute-start.3
  57.4 16.7 %collective-permute-done.3 = bf16[256,576]{1,0:T(8,128)(2,1)} collective-permute-done((bf16[256,576]{1,0:T(8,128)(2,1)S(1)}, bf16[256,576]{1,0:T(8,128)(2,1)}, u32[]{:S(2)}, u32[]{:S(2)}) %collective-permute-start.3) | collective-permute-done | bytes 294944 | tf_op jit(solution)/shard_map/cond/branch_3_fun/ppermute | solution.py:24
  74.1 0.0 copy-done.7
  74.1 0.1 convert_reduce_fusion
  74.2 1.2 %pad_maximum_fusion = bf16[2,256,576]{2,1,0:T(8,128)(2,1)S(1)} fusion(bf16[1,256,576]{2,1,0:T(8,128)(2,1)} %get-tuple-element.231, bf16[1,256,576]{2,1,0:T(8,128)(2,1)} %get-tuple-element.230), kind=kLoop, calls=%fused_computation.35 | loop fusion | flops 294912 | bytes 1179648 | tf_op jit(solution)/shard_map/stack | solution.py:94
  75.4 0.2 copy.67
  75.6 0.0 copy-start.9
  75.6 14.2 %psum.7 = f32[8]{0:T(128)} all-reduce(f32[8]{0:T(128)S(1)} %bitcast_add_fusion), channel_id=1, replica_groups=mesh['grp'=4,'dev'=8] {'dev'}, use_global_device_ids=true, to_apply=%region_23.24 | all-reduce | flops 8 | bytes 64 | tf_op jit(solution)/shard_map/psum | solution.py:105
  89.8 0.8 scatter_fusion
  90.6 0.0 copy-start
  90.6 0.7 dynamic-slice
  92.0 0.8 divide_convert_fusion
  92.8 11.5 %all-reduce.3.cloned.1.call-done = f32[32,3584]{1,0:T(8,128)} async-done(((f32[32,3584]{1,0:T(8,128)}), f32[32,3584]{1,0:T(8,128)}) %all-reduce.3.cloned.1.call-update) | async-done | bytes 458768
  104.3 1.5 %fusion.18 = bf16[4,3584]{1,0:T(4,128)(2,1)} fusion(bf16[4,3584]{1,0:T(4,128)(2,1)S(1)} %copy-done.3, f32[32,3584]{1,0:T(8,128)} %all-reduce.3.cloned.1.call-done, u32[]{:T(128)S(6)} %multiply.7), kind=kLoop, calls=%fused_computation.46 | loop fusion | flops 43008 | bytes 114692 | tf_op jit(solution)/shard_map/convert_element_type | solution.py:115
  (21 shorter events, 0.1 us)
Async XLA Ops:
  7.2 0.7 copy-start.3
  7.2 0.7 copy-start.4
  7.2 97.2 %all-reduce.3.cloned.1.call-start = ((), (), s32[]{:S(2)}) async-start(), calls=%async_computation | async-start | bytes 917504
  24.2 10.5 %copy-start.6 = (s32[32]{0:T(128)S(1)}, s32[32]{0:T(128)}, u32[]{:S(2)}) copy-start(s32[32]{0:T(128)} %param.28) | copy-start | bytes 388
  24.2 12.0 %copy-start.1 = (bf16[4,256,576]{1,2,0:T(8,128)(2,1)S(1)}, bf16[4,256,576]{1,2,0:T(8,128)(2,1)}, u32[]{:S(2)}) copy-start(bf16[4,256,576]{1,2,0:T(8,128)(2,1)} %param.27) | copy-start | bytes 3538948
  24.2 12.0 %copy-start.2 = (bf16[4,64,576]{2,1,0:T(8,128)(2,1)S(1)}, bf16[4,64,576]{2,1,0:T(8,128)(2,1)}, u32[]{:S(2)}) copy-start(bf16[4,64,576]{2,1,0:T(8,128)(2,1)} %param.26) | copy-start | bytes 884740
  36.2 1.1 copy-start.5
  40.6 16.7 %collective-permute-start.9 = (bf16[256,576]{1,0:T(8,128)(2,1)S(1)}, bf16[256,576]{1,0:T(8,128)(2,1)}, u32[]{:S(2)}, u32[]{:S(2)}) collective-permute-start(bf16[256,576]{1,0:T(8,128)(2,1)S(1)} %slice_bitcast_fusion.9), channel_id=1, source_target_pairs={{0,3},{1,4},{2,5},{3,6},{4,7},{5,0},{6,1},{7,2},{8,11},{9,12},{10,... | collective-permute-start | bytes 884744 | tf_op jit(solution)/shard_map/cond/branch_2_fun/ppermute | solution.py:24
  57.2 16.8 %copy-start.7 = (s32[4]{0:T(128)S(1)}, s32[4]{0:T(128)}, u32[]{:S(2)}) copy-start(s32[4]{0:T(128)} %param.35) | copy-start | bytes 52
  57.3 16.8 %collective-permute-start.3 = (bf16[256,576]{1,0:T(8,128)(2,1)S(1)}, bf16[256,576]{1,0:T(8,128)(2,1)}, u32[]{:S(2)}, u32[]{:S(2)}) collective-permute-start(bf16[256,576]{1,0:T(8,128)(2,1)S(1)} %slice_bitcast_fusion.3), channel_id=1, source_target_pairs={{0,4},{1,5},{2,6},{3,7},{4,0},{5,1},{6,2},{7,3},{8,12},{9,13},{10,... | collective-permute-start | bytes 884744 | tf_op jit(solution)/shard_map/cond/branch_3_fun/ppermute | solution.py:24
  74.1 1.3 %copy-start.8 = (s32[1,8]{1,0:T(1,128)S(1)}, s32[1,8]{1,0:T(1,128)}, u32[]{:S(2)}) copy-start(s32[1,8]{1,0:T(1,128)} %param.34) | copy-start | bytes 100
  75.6 15.0 %copy-start.9 = (u32[32]{0:T(128)S(1)}, u32[32]{0:T(128)}, u32[]{:S(2)}) copy-start(u32[32]{0:T(128)} %constant.94) | copy-start | bytes 388
  90.6 15.3 %copy-start = (bf16[4,256,576]{1,2,0:T(8,128)(2,1)}, bf16[4,256,576]{1,2,0:T(8,128)(2,1)S(1)}, u32[]{:S(2)}) copy-start(bf16[4,256,576]{1,2,0:T(8,128)(2,1)S(1)} %scatter_fusion) | copy-start | bytes 3538948
Sparse Core Ops, SparseCore 0:
  34.8 69.4 all-reduce.2
where the time goes:
time: 113 us
  waiting for transfers between devices  42.4 us (38%)
  blocking collectives  30.2 us (27%)
  between operations  16.9 us (15%)
  matrix products  11.1 us (10%)
  other arithmetic  5.04 us (4%)
  local copies, waits for them, and re-layouts  4.32 us (4%)
  starting transfers between devices  2.65 us (2%)
    ppermute x2, waiting for transfers between devices, shifted(): return lax.ppermute(value, axis, pairs)  30.8 us
    all_gather x1, blocking collectives, per_device(): all_rows = lax.all_gather(normed, 'dev', axis=0, tiled=True)  16 us
    psum x1, blocking collectives, per_device(): bucket_load = lax.psum(bucket_terms, 'dev')  14.2 us
    unnamed x2, waiting for transfers between devices  11.6 us
    dot_general x1, matrix products, per_device(): jnp.dot(hidden_units, w_down, preferred_element_type=jnp.float32)  10.4 us
    ppermute x2, starting transfers between devices, shifted(): return lax.ppermute(value, axis, pairs)  2.61 us
  transfers between devices with their start and end apart: 3, of which 3 were waited for; matrix products, arithmetic and copies ran while one was open for 7% of the time, Pallas kernels for 0%

commit v1 on v0

--- a/solution.py
+++ b/solution.py
@@ -1,3 +1,4 @@
+import functools
 from functools import partial
 import jax
 import jax.numpy as jnp
@@ -8,6 +9,24 @@
 MOVE_DEV = 2
 BUCKETS = 8
 softmax_scale = 192.0 ** (-0.5)
+
+
+def fill_lots_all_here(local_x, where_dim):
+    parts_n = lax.axis_size("dev")
+    block_out = local_x
+    table = [block_out]
+    y1 = [(j0 - 1, j0) for j0 in range(1, parts_n)] + [(parts_n - 1, 0)]
+    for _ in range(parts_n - 1):
+        block_out = lax.ppermute(block_out, axis_name="dev", perm=y1)
+        table += [block_out]
+    return jnp.roll(
+        jnp.concatenate([*reversed(table)], axis=where_dim),
+        (lax.axis_index("dev") + 1) * block_out.shape[where_dim],
+        axis=where_dim,
+    )
+
+
+expand_the_corner = functools.partial(fill_lots_all_here, where_dim=0)
 
 
 def for_sending(x):
@@ -101,7 +120,7 @@
         jnp.float32
     )
     bucket_terms = queue_counts.astype(jnp.float32)[0] + jnp.sum(running, axis=0)
-    all_rows = lax.all_gather(normed, "dev", axis=0, tiled=True)
+    all_rows = expand_the_corner(normed)
     bucket_load = lax.psum(bucket_terms, "dev")
     hidden_units = jax.nn.silu(jnp.dot(all_rows, w_up, preferred_element_type=jnp.float32)).astype(
         jnp.bfloat16

time: 113 us -> 159 us (1.41)
  waiting for transfers between devices: 42.4 us -> 103 us
  blocking collectives: 30.2 us -> 17.6 us
  starting transfers between devices: 2.65 us -> 0.73 us
    unnamed x2, waiting for transfers between devices: 11.6 us -> 53.4 us
    ppermute x0 -> x7, waiting for transfers between devices: none -> 22.2 us  [fill_lots_all_here(): block_out = lax.ppermute(block_out, axis_name='dev', perm=y1)]
    all_gather x1 -> x0, blocking collectives: 16 us -> none  [per_device(): all_rows = lax.all_gather(normed, 'dev', axis=0, tiled=True)]
    ppermute x2, waiting for transfers between devices: 30.8 us -> 26.8 us  [shifted(): return lax.ppermute(value, axis, pairs)]
    psum x1, blocking collectives: 14.2 us -> 17.6 us  [per_device(): bucket_load = lax.psum(bucket_terms, 'dev')]
    ppermute x2, starting transfers between devices: 2.61 us -> 0.13 us  [shifted(): return lax.ppermute(value, axis, pairs)]
  transfers between devices with their start and end apart: 3 -> 10, of which waited for: 3 -> 8; matrix products, arithmetic and copies ran while one was open for 7% -> 5% of each run, Pallas kernels for 0% -> 0%
where the time goes in v1:
time: 159 us
  waiting for transfers between devices  103 us (65%)
  blocking collectives  17.6 us (11%)
  between operations  16.9 us (11%)
  matrix products  11 us (7%)
  other arithmetic  5.03 us (3%)
  local copies, waits for them, and re-layouts  4.73 us (3%)
    unnamed x2, waiting for transfers between devices  53.4 us
    ppermute x2, waiting for transfers between devices, shifted(): return lax.ppermute(value, axis, pairs)  26.8 us
    ppermute x7, waiting for transfers between devices, fill_lots_all_here(): block_out = lax.ppermute(block_out, axis_name='dev', perm=y1)  22.2 us
    psum x1, blocking collectives, per_device(): bucket_load = lax.psum(bucket_terms, 'dev')  17.6 us
    dot_general x1, matrix products, per_device(): jnp.dot(hidden_units, w_down, preferred_element_type=jnp.float32)  10.3 us
  transfers between devices with their start and end apart: 10, of which 8 were waited for; matrix products, arithmetic and copies ran while one was open for 5% of the time, Pallas kernels for 0%

profile of v1, /device:TPU:0, one launch (start us, length us, event | category | flops | bytes accessed | tf_op | source)
XLA Modules:
  0.0 158.6 jit_solution(8248070877447756012)
XLA Ops:
  7.2 0.0 all-reduce.3.cloned.1.call-start
  7.3 0.8 copy-done.4
  8.0 0.0 copy-done.3
  8.1 0.1 fusion.21
  8.2 0.1 fusion.23
  8.3 0.5 collective-permute-start.14
  8.9 0.7 fusion.30
  10.3 0.1 broadcast_in_dim.42
  10.3 0.0 copy-start.7
  10.3 0.0 copy-start.8
  10.4 0.0 copy-start.5
  10.4 1.0 while.14
  10.4 0.1 broadcast_compare_fusion.2
  10.5 0.3 fusion.44
  10.8 0.2 fusion.45
  11.0 0.4 convolution_add_fusion.2
  11.4 0.1 convert_reduce_fusion
  11.5 0.1 reshape.69
  11.6 2.8 %collective-permute-done.14 = bf16[4,3584]{1,0:T(4,128)(2,1)S(1)} collective-permute-done((bf16[4,3584]{1,0:T(4,128)(2,1)S(1)}, bf16[4,3584]{1,0:T(4,128)(2,1)S(1)}, u32[]{:S(2)}, u32[]{:S(2)}) %collective-permute-start.14) | collective-permute-done | bytes 28704 | tf_op jit(solution)/shard_map/ppermute | solution.py:20
  14.4 0.1 constant_dynamic-slice_fusion
  14.5 0.1 copy.52
  14.6 4.9 %collective-permute-done.15 = bf16[4,3584]{1,0:T(4,128)(2,1)S(1)} collective-permute-done((bf16[4,3584]{1,0:T(4,128)(2,1)S(1)}, bf16[4,3584]{1,0:T(4,128)(2,1)S(1)}, u32[]{:S(2)}, u32[]{:S(2)}) %collective-permute-start.15) | collective-permute-done | bytes 28704 | tf_op jit(solution)/shard_map/ppermute | solution.py:20
  19.5 0.2 subtract_reduce_fusion
  19.7 4.9 %collective-permute-done.16 = bf16[4,3584]{1,0:T(4,128)(2,1)S(1)} collective-permute-done((bf16[4,3584]{1,0:T(4,128)(2,1)S(1)}, bf16[4,3584]{1,0:T(4,128)(2,1)S(1)}, u32[]{:S(2)}, u32[]{:S(2)}) %collective-permute-start.16) | collective-permute-done | bytes 28704 | tf_op jit(solution)/shard_map/ppermute | solution.py:20
  24.6 5.1 %collective-permute-done.17 = bf16[4,3584]{1,0:T(4,128)(2,1)S(1)} collective-permute-done((bf16[4,3584]{1,0:T(4,128)(2,1)S(1)}, bf16[4,3584]{1,0:T(4,128)(2,1)S(1)}, u32[]{:S(2)}, u32[]{:S(2)}) %collective-permute-start.17) | collective-permute-done | bytes 28704 | tf_op jit(solution)/shard_map/ppermute | solution.py:20
  29.7 0.6 fusion.32
  30.3 4.5 %collective-permute-done.18 = bf16[4,3584]{1,0:T(4,128)(2,1)S(1)} collective-permute-done((bf16[4,3584]{1,0:T(4,128)(2,1)S(1)}, bf16[4,3584]{1,0:T(4,128)(2,1)S(1)}, u32[]{:S(2)}, u32[]{:S(2)}) %collective-permute-start.18) | collective-permute-done | bytes 28704 | tf_op jit(solution)/shard_map/ppermute | solution.py:20
  34.8 0.6 gather_fusion
  35.4 0.3 copy.53
  37.0 12.4 %conditional.3 = (bf16[1,256,576]{2,1,0:T(8,128)(2,1)}) conditional(s32[]{:T(128)} %bitcast.31, bf16[2,256,576]{2,1,0:T(8,128)(2,1)S(1)} %copy.53, bf16[2,256,576]{2,1,0:T(8,128)(2,1)S(1)} %copy.53, bf16[2,256,576]{2,1,0:T(8,128)(2,1)S(1)} %copy.53, bf16[2,256,576]{2,1,0:T(8,128)(2,1)S(1)} %copy.53, ...), branch_computations={%region_12.13_spmd, %region_13.14_spmd, %region_14.15_spmd, %regio... | conditional | bytes 1769520 | solution.py:94
  37.1 0.1 collective-permute-start.9
  37.2 12.3 %collective-permute-done.9 = bf16[256,576]{1,0:T(8,128)(2,1)} collective-permute-done((bf16[256,576]{1,0:T(8,128)(2,1)S(1)}, bf16[256,576]{1,0:T(8,128)(2,1)}, u32[]{:S(2)}, u32[]{:S(2)}) %collective-permute-start.9) | collective-permute-done | bytes 294944 | tf_op jit(solution)/shard_map/cond/branch_2_fun/ppermute | solution.py:43
  49.5 14.7 %conditional.2 = (bf16[1,256,576]{2,1,0:T(8,128)(2,1)}) conditional(s32[]{:T(128)} %bitcast.30, bf16[2,256,576]{2,1,0:T(8,128)(2,1)S(1)} %copy.53, bf16[2,256,576]{2,1,0:T(8,128)(2,1)S(1)} %copy.53, bf16[2,256,576]{2,1,0:T(8,128)(2,1)S(1)} %copy.53, bf16[2,256,576]{2,1,0:T(8,128)(2,1)S(1)} %copy.53, ...), branch_computations={%region_5.6_spmd, %region_6.7_spmd, %region_7.8_spmd, %region_8.9_... | conditional | bytes 1769520 | solution.py:94
  49.5 0.1 collective-permute-start.3
  49.6 14.5 %collective-permute-done.3 = bf16[256,576]{1,0:T(8,128)(2,1)} collective-permute-done((bf16[256,576]{1,0:T(8,128)(2,1)S(1)}, bf16[256,576]{1,0:T(8,128)(2,1)}, u32[]{:S(2)}, u32[]{:S(2)}) %collective-permute-start.3) | collective-permute-done | bytes 294944 | tf_op jit(solution)/shard_map/cond/branch_3_fun/ppermute | solution.py:43
  64.1 1.2 pad_maximum_fusion
  65.3 17.6 %psum.7 = f32[8]{0:T(128)} all-reduce(f32[8]{0:T(128)S(1)} %bitcast_add_fusion), channel_id=1, replica_groups=mesh['grp'=4,'dev'=8] {'dev'}, use_global_device_ids=true, to_apply=%region_23.24 | all-reduce | flops 8 | bytes 64 | tf_op jit(solution)/shard_map/psum | solution.py:124
  82.9 0.2 copy.67
  83.2 0.0 copy-start.9
  83.2 0.8 scatter_fusion
  84.0 0.0 copy-start
  84.0 0.7 dynamic-slice
  85.4 0.4 concatenate.6
  85.7 10.3 %fusion.18 = f32[32,3584]{1,0:T(8,128)} fusion(bf16[1280,3584]{1,0:T(8,128)(2,1)} %param.33, bf16[3584,1280]{1,0:T(8,128)(2,1)} %param.32, bf16[64,3584]{1,0:T(8,128)(2,1)S(1)} %concatenate.6, s32[]{:T(128)S(6)} %select_n.53), kind=kOutput, calls=%fused_computation.40 | convolution fusion | flops 587407360 | bytes 19038212 | tf_op jit(solution)/shard_map/dot_general | solution.py:129
  96.0 0.0 all-reduce.3.cloned.1.call-update
  96.0 0.8 divide_convert_fusion
  96.8 53.4 %all-reduce.3.cloned.1.call-done = f32[32,3584]{1,0:T(8,128)} async-done(((f32[32,3584]{1,0:T(8,128)}), f32[32,3584]{1,0:T(8,128)}) %all-reduce.3.cloned.1.call-update) | async-done | bytes 458768
  150.2 1.5 fusion.24
  (34 shorter events, 0.2 us)
Async XLA Ops:
  7.2 3.2 %copy-start.2 = (bf16[4,64,576]{2,1,0:T(8,128)(2,1)S(1)}, bf16[4,64,576]{2,1,0:T(8,128)(2,1)}, u32[]{:S(2)}) copy-start(bf16[4,64,576]{2,1,0:T(8,128)(2,1)} %param.26) | copy-start | bytes 884740
  7.2 3.2 %copy-start.1 = (bf16[4,256,576]{1,2,0:T(8,128)(2,1)S(1)}, bf16[4,256,576]{1,2,0:T(8,128)(2,1)}, u32[]{:S(2)}) copy-start(bf16[4,256,576]{1,2,0:T(8,128)(2,1)} %param.27) | copy-start | bytes 3538948
  7.2 1.7 %copy-start.6 = (s32[32]{0:T(128)S(1)}, s32[32]{0:T(128)}, u32[]{:S(2)}) copy-start(s32[32]{0:T(128)} %param.28) | copy-start | bytes 388
  7.2 0.9 copy-start.3
  7.2 0.8 copy-start.4
  7.2 143.0 %all-reduce.3.cloned.1.call-start = ((), (), s32[]{:S(2)}) async-start(), calls=%async_computation | async-start | bytes 917504
  8.3 6.1 %collective-permute-start.14 = (bf16[4,3584]{1,0:T(4,128)(2,1)S(1)}, bf16[4,3584]{1,0:T(4,128)(2,1)S(1)}, u32[]{:S(2)}, u32[]{:S(2)}) collective-permute-start(bf16[4,3584]{1,0:T(4,128)(2,1)S(1)} %fusion.23), channel_id=1, source_target_pairs={{0,1},{1,2},{2,3},{3,4},{4,5},{5,6},{6,7},{7,0},{8,9},{9,10},{10,1... | collective-permute-start | bytes 86024 | tf_op jit(solution)/shard_map/ppermute | solution.py:20
  10.3 1.1 copy-start.7
  10.3 1.2 copy-start.8
  10.4 1.2 copy-start.5
  14.4 5.1 %collective-permute-start.15 = (bf16[4,3584]{1,0:T(4,128)(2,1)S(1)}, bf16[4,3584]{1,0:T(4,128)(2,1)S(1)}, u32[]{:S(2)}, u32[]{:S(2)}) collective-permute-start(bf16[4,3584]{1,0:T(4,128)(2,1)S(1)} %collective-permute-done.14), channel_id=1, source_target_pairs={{0,1},{1,2},{2,3},{3,4},{4,5},{5,6},{6,7},{7,0},{8,9},{9,10},{10,1... | collective-permute-start | bytes 86024 | tf_op jit(solution)/shard_map/ppermute | solution.py:20
  19.5 5.1 %collective-permute-start.16 = (bf16[4,3584]{1,0:T(4,128)(2,1)S(1)}, bf16[4,3584]{1,0:T(4,128)(2,1)S(1)}, u32[]{:S(2)}, u32[]{:S(2)}) collective-permute-start(bf16[4,3584]{1,0:T(4,128)(2,1)S(1)} %collective-permute-done.15), channel_id=1, source_target_pairs={{0,1},{1,2},{2,3},{3,4},{4,5},{5,6},{6,7},{7,0},{8,9},{9,10},{10,1... | collective-permute-start | bytes 86024 | tf_op jit(solution)/shard_map/ppermute | solution.py:20
  24.6 5.1 %collective-permute-start.17 = (bf16[4,3584]{1,0:T(4,128)(2,1)S(1)}, bf16[4,3584]{1,0:T(4,128)(2,1)S(1)}, u32[]{:S(2)}, u32[]{:S(2)}) collective-permute-start(bf16[4,3584]{1,0:T(4,128)(2,1)S(1)} %collective-permute-done.16), channel_id=1, source_target_pairs={{0,1},{1,2},{2,3},{3,4},{4,5},{5,6},{6,7},{7,0},{8,9},{9,10},{10,1... | collective-permute-start | bytes 86024 | tf_op jit(solution)/shard_map/ppermute | solution.py:20
  29.7 5.1 %collective-permute-start.18 = (bf16[4,3584]{1,0:T(4,128)(2,1)S(1)}, bf16[4,3584]{1,0:T(4,128)(2,1)S(1)}, u32[]{:S(2)}, u32[]{:S(2)}) collective-permute-start(bf16[4,3584]{1,0:T(4,128)(2,1)S(1)} %collective-permute-done.17), channel_id=1, source_target_pairs={{0,1},{1,2},{2,3},{3,4},{4,5},{5,6},{6,7},{7,0},{8,9},{9,10},{10,1... | collective-permute-start | bytes 86024 | tf_op jit(solution)/shard_map/ppermute | solution.py:20
  34.8 29.3 %collective-permute-start.19 = (bf16[4,3584]{1,0:T(4,128)(2,1)S(1)}, bf16[4,3584]{1,0:T(4,128)(2,1)S(1)}, u32[]{:S(2)}, u32[]{:S(2)}) collective-permute-start(bf16[4,3584]{1,0:T(4,128)(2,1)S(1)} %collective-permute-done.18), channel_id=1, source_target_pairs={{0,1},{1,2},{2,3},{3,4},{4,5},{5,6},{6,7},{7,0},{8,9},{9,10},{10,1... | collective-permute-start | bytes 86024 | tf_op jit(solution)/shard_map/ppermute | solution.py:20
  37.1 12.4 %collective-permute-start.9 = (bf16[256,576]{1,0:T(8,128)(2,1)S(1)}, bf16[256,576]{1,0:T(8,128)(2,1)}, u32[]{:S(2)}, u32[]{:S(2)}) collective-permute-start(bf16[256,576]{1,0:T(8,128)(2,1)S(1)} %slice_bitcast_fusion.9), channel_id=1, source_target_pairs={{0,3},{1,4},{2,5},{3,6},{4,7},{5,0},{6,1},{7,2},{8,11},{9,12},{10,... | collective-permute-start | bytes 884744 | tf_op jit(solution)/shard_map/cond/branch_2_fun/ppermute | solution.py:43
  49.5 14.6 %collective-permute-start.3 = (bf16[256,576]{1,0:T(8,128)(2,1)S(1)}, bf16[256,576]{1,0:T(8,128)(2,1)}, u32[]{:S(2)}, u32[]{:S(2)}) collective-permute-start(bf16[256,576]{1,0:T(8,128)(2,1)S(1)} %slice_bitcast_fusion.3), channel_id=1, source_target_pairs={{0,4},{1,5},{2,6},{3,7},{4,0},{5,1},{6,2},{7,3},{8,12},{9,13},{10,... | collective-permute-start | bytes 884744 | tf_op jit(solution)/shard_map/cond/branch_3_fun/ppermute | solution.py:43
  64.1 21.2 %collective-permute-start.20 = (bf16[4,3584]{1,0:T(4,128)(2,1)S(1)}, bf16[4,3584]{1,0:T(4,128)(2,1)S(1)}, u32[]{:S(2)}, u32[]{:S(2)}) collective-permute-start(bf16[4,3584]{1,0:T(4,128)(2,1)S(1)} %collective-permute-done.19), channel_id=1, source_target_pairs={{0,1},{1,2},{2,3},{3,4},{4,5},{5,6},{6,7},{7,0},{8,9},{9,10},{10,1... | collective-permute-start | bytes 86024 | tf_op jit(solution)/shard_map/ppermute | solution.py:20
  83.2 0.8 copy-start.9
  84.0 12.0 %copy-start = (bf16[4,256,576]{1,2,0:T(8,128)(2,1)}, bf16[4,256,576]{1,2,0:T(8,128)(2,1)S(1)}, u32[]{:S(2)}) copy-start(bf16[4,256,576]{1,2,0:T(8,128)(2,1)S(1)} %scatter_fusion) | copy-start | bytes 3538948
Sparse Core Ops, SparseCore 0:
  96.1 54.0 all-reduce.2
